TPU v7x, 32 devices: a whole 2x2x4 slice. The times are simulated.
32 devices in a mesh: section: 2 (over y), seq: 16 (over z, x, core).
Axes of the slice: x: 2, y: 2, z: 4, core: 2. Of those that a mesh axis runs over, the one named last changes fastest.
Arguments:
- queries: bfloat16 [2, 2048, 1024], P('section', 'seq'), may hold values from -35 to 35
- keys: bfloat16 [2, 2048, 1024], P('section', 'seq'), may hold values from -4 to 4
- values: bfloat16 [2, 2048, 1024], P('section', 'seq'), may hold values from -6 to 6
- upstream: bfloat16 [2, 2048, 1024], P('section', 'seq'), may hold values from -6 to 6
- neighbours: int32 [16, 6], replicated, may hold values from 0 to 15, as said below
- counts: int32 [16], replicated, may hold values from 1 to 6, as said below
Outputs:
- query_grad: bfloat16 [2, 2048, 1024], P('section', 'seq')
- key_grad: bfloat16 [2, 2048, 1024], P('section', 'seq')
- value_grad: bfloat16 [2, 2048, 1024], P('section', 'seq')
Inputs may be any that keep to these rules, and one draw needn't show every extreme that they name: Row a lists 6 different tiles, the first being a itself; only the first counts[a] of them are neighbours of a. `counts`: some tile has 6 neighbour tiles and some tile has only itself.
All inputs are finite; a program needn't handle non-finite values.
Results may differ from a plain program's by a relative error of at most 0.009.
Values may be sent and summed in bfloat16 or wider, within the bound.
A program may use at most 64 MiB of HBM per device.

v0:
```python
import jax
import jax.numpy as jnp
from jax import lax
from jax.sharding import PartitionSpec as P

HEADS = 16
DH = 64
TILE = 128
MAXNB = 6
MASKED = -1e30


def from_behind(block, axis, distance):
    devices = range(lax.axis_size(axis))
    route = [((i - distance) % len(devices), i) for i in devices]
    return lax.ppermute(block, axis, route)


def per_device(queries, keys, values, upstream, neighbours, counts):
    seq_count = lax.axis_size("seq")
    group_count = seq_count // HEADS
    row_count = queries.shape[1]
    model_width = queries.shape[2]
    quarter_rows = row_count // group_count
    unit_rows = min(quarter_rows, TILE)
    tile_count = neighbours.shape[0]
    my_group = lax.axis_index("seq") // HEADS
    adjoint = from_behind(upstream, "section", -1)

    def to_slots(block):
        return (
            block[0]
            .reshape(group_count, quarter_rows, HEADS, DH)
            .transpose(0, 2, 3, 1)
            .reshape(group_count * HEADS, DH, quarter_rows)
        )

    query_recv, adjoint_recv = (
        lax.all_to_all(to_slots(queries), "seq", split_axis=0, concat_axis=2, tiled=True),
        lax.all_to_all(to_slots(adjoint), "seq", split_axis=0, concat_axis=2, tiled=True),
    )
    query_cols = query_recv[0]
    adjoint_cols = adjoint_recv[0]

    def spread_rows(block):
        heads_first = block[0].reshape(row_count, HEADS, DH).transpose(1, 2, 0)
        return jnp.broadcast_to(heads_first[None], (group_count, HEADS, DH, row_count)).reshape(
            group_count * HEADS, DH, row_count
        )

    key_recv, value_recv = (
        lax.all_to_all(spread_rows(keys), "seq", split_axis=0, concat_axis=2, tiled=True),
        lax.all_to_all(spread_rows(values), "seq", split_axis=0, concat_axis=2, tiled=True),
    )
    key_cols = key_recv[0]
    value_cols = value_recv[0]
    key_tiles = key_cols.reshape(DH, tile_count, TILE).transpose(1, 0, 2)
    value_tiles = value_cols.reshape(DH, tile_count, TILE).transpose(1, 0, 2)
    query_total = seq_count * quarter_rows
    unit_count = query_total // unit_rows
    per_batch = min(unit_count, max(1, 512 // unit_rows))
    batch_count = unit_count // per_batch
    first_row = jnp.arange(unit_count, dtype=jnp.int32) * unit_rows
    source = first_row // quarter_rows
    offset = first_row % quarter_rows
    global_row = source * row_count + my_group * quarter_rows + offset
    unit_tiles = (global_row // TILE).reshape(batch_count, per_batch)

    def by_unit(cols):
        return cols.reshape(DH, batch_count, per_batch, unit_rows).transpose(1, 2, 0, 3)

    valid_table = (jnp.arange(MAXNB, dtype=jnp.int32)[None, :] < counts[:, None]).astype(
        jnp.float32
    )
    score_scale = DH ** (-0.5)
    tile_numbers = jnp.arange(tile_count, dtype=jnp.int32)

    def tile_sweep(carried, inputs):
        key_acc, value_acc = carried
        query_blk, adjoint_blk, tile_ids = inputs
        chosen = neighbours[tile_ids]
        alive_slots = valid_table[tile_ids][:, :, None, None]
        key_blk = key_tiles[chosen]
        value_blk = value_tiles[chosen]
        scores = (
            jnp.einsum("bei,bsej->bsij", query_blk, key_blk, preferred_element_type=jnp.float32)
            * score_scale
        )
        scores = jnp.where(alive_slots > 0, scores, MASKED)
        row_peak = jnp.max(scores, axis=(1, 3), keepdims=True)
        weights = jnp.exp(scores - row_peak) * alive_slots
        prob_full = weights / jnp.sum(weights, axis=(1, 3), keepdims=True)
        probs_low = prob_full.astype(jnp.bfloat16)
        dprobs = jnp.einsum(
            "bei,bsej->bsij", adjoint_blk, value_blk, preferred_element_type=jnp.float32
        )
        delta_sum = jnp.sum(prob_full * dprobs, axis=(1, 3), keepdims=True)
        dscores = (prob_full * (dprobs - delta_sum) * score_scale).astype(jnp.bfloat16)
        query_out = jnp.einsum(
            "bsij,bsej->bei", dscores, key_blk, preferred_element_type=jnp.float32
        ).astype(jnp.bfloat16)
        key_terms = jnp.einsum(
            "bsij,bei->bsej", dscores, query_blk, preferred_element_type=jnp.float32
        )
        value_terms = jnp.einsum(
            "bsij,bei->bsej", probs_low, adjoint_blk, preferred_element_type=jnp.float32
        )
        flat_ids = chosen.reshape(-1)
        picker = (flat_ids[None, :] == tile_numbers[:, None]).astype(jnp.float32)
        key_acc = key_acc + jnp.einsum(
            "tn,nej->tej",
            picker,
            key_terms.reshape(-1, DH, TILE),
            precision=lax.Precision.HIGHEST,
            preferred_element_type=jnp.float32,
        )
        value_acc = value_acc + jnp.einsum(
            "tn,nej->tej",
            picker,
            value_terms.reshape(-1, DH, TILE),
            precision=lax.Precision.HIGHEST,
            preferred_element_type=jnp.float32,
        )
        return ((key_acc, value_acc), query_out)

    empty_grad = jnp.zeros((tile_count, DH, TILE), jnp.float32)
    (key_acc, value_acc), query_units = lax.scan(
        tile_sweep,
        (empty_grad, empty_grad),
        (by_unit(query_cols), by_unit(adjoint_cols), unit_tiles),
    )
    query_send = (
        query_units.reshape(seq_count, quarter_rows // unit_rows, DH, unit_rows)
        .transpose(0, 2, 1, 3)
        .reshape(seq_count, 1, DH, quarter_rows)
    )
    query_back = lax.all_to_all(query_send, "seq", split_axis=0, concat_axis=1, tiled=True)
    query_grad = (
        query_back[0]
        .reshape(group_count, HEADS, DH, quarter_rows)
        .transpose(0, 3, 1, 2)
        .reshape(1, row_count, model_width)
    )

    def by_source(grad):
        return (
            grad.reshape(seq_count, row_count // TILE, DH, TILE)
            .transpose(0, 2, 1, 3)
            .reshape(seq_count, 1, DH, row_count)
        )

    got_key, got_value = (
        lax.all_to_all(
            by_source(key_acc).astype(jnp.bfloat16), "seq", split_axis=0, concat_axis=1, tiled=True
        ).astype(jnp.float32),
        lax.all_to_all(
            by_source(value_acc).astype(jnp.bfloat16),
            "seq",
            split_axis=0,
            concat_axis=1,
            tiled=True,
        ).astype(jnp.float32),
    )

    def finish_rows(got):
        summed = jnp.sum(got[0].reshape(group_count, HEADS, DH, row_count), axis=0)
        return summed.transpose(2, 0, 1).reshape(1, row_count, model_width).astype(jnp.bfloat16)

    key_grad = finish_rows(got_key)
    value_grad = finish_rows(got_value)
    return (query_grad, key_grad, value_grad)


def solution(mesh):
    in_specs = (
        P("section", "seq", None),
        P("section", "seq", None),
        P("section", "seq", None),
        P("section", "seq", None),
        P(),
        P(),
    )
    out_specs = (P("section", "seq", None), P("section", "seq", None), P("section", "seq", None))
    return jax.shard_map(
        per_device, mesh=mesh, in_specs=in_specs, out_specs=out_specs, check_vma=False
    )
```

profile of v0, /device:TPU:0, one launch (start us, length us, event | category | flops | bytes accessed | tf_op | source)
XLA Modules:
  0.0 162.7 jit_solution(16621503994922736800)
XLA Ops:
  0.7 1.8 %copy.46 = bf16[1,128,1024]{1,2,0:T(8,128)(2,1)} copy(bf16[1,128,1024]{2,1,0:T(8,128)(2,1)} %param.9) | data formatting | bytes 524288 | tf_op args[1]
  2.5 7.4 %all-to-all-start.1 = ((bf16[16,64,128]{2,1,0:T(8,128)(2,1)}), bf16[16,64,128]{2,1,0:T(8,128)(2,1)S(1)}, u32[]{:S(2)}, u32[]{:S(2)}) async-start(bf16[16,64,128]{2,1,0:T(8,128)(2,1)} %bitcast.8), calls=%async_computation.1 | async-start | bytes 524288 | tf_op jit(solution)/shard_map/all_to_all | solution.py:52
  9.9 1.8 %copy.47 = bf16[1,128,1024]{1,2,0:T(8,128)(2,1)} copy(bf16[1,128,1024]{2,1,0:T(8,128)(2,1)} %param.10) | data formatting | bytes 524288 | tf_op args[2]
  11.7 8.2 %all-to-all-done.1 = bf16[16,64,128]{2,1,0:T(8,128)(2,1)S(1)} async-done(((bf16[16,64,128]{2,1,0:T(8,128)(2,1)}), bf16[16,64,128]{2,1,0:T(8,128)(2,1)S(1)}, u32[]{:S(2)}, u32[]{:S(2)}) %all-to-all-start.1) | async-done | bytes 262176 | tf_op jit(solution)/shard_map/all_to_all | solution.py:52
  19.9 3.5 %all-to-all-start.2 = ((bf16[16,64,128]{2,1,0:T(8,128)(2,1)}), bf16[16,64,128]{2,1,0:T(8,128)(2,1)S(1)}, u32[]{:S(2)}, u32[]{:S(2)}) async-start(bf16[16,64,128]{2,1,0:T(8,128)(2,1)} %bitcast.10), calls=%async_computation.2 | async-start | bytes 524288 | tf_op jit(solution)/shard_map/all_to_all | solution.py:53
  23.5 0.8 copy.45
  24.3 9.1 %all-to-all-done.2 = bf16[16,64,128]{2,1,0:T(8,128)(2,1)S(1)} async-done(((bf16[16,64,128]{2,1,0:T(8,128)(2,1)}), bf16[16,64,128]{2,1,0:T(8,128)(2,1)S(1)}, u32[]{:S(2)}, u32[]{:S(2)}) %all-to-all-start.2) | async-done | bytes 262176 | tf_op jit(solution)/shard_map/all_to_all | solution.py:53
  33.4 3.5 %all-to-all-start = ((bf16[16,64,128]{2,1,0:T(8,128)(2,1)}), bf16[16,64,128]{2,1,0:T(8,128)(2,1)S(1)}, u32[]{:S(2)}, u32[]{:S(2)}) async-start(bf16[16,64,128]{2,1,0:T(8,128)(2,1)} %bitcast.2), calls=%async_computation | async-start | bytes 524288 | tf_op jit(solution)/shard_map/all_to_all | solution.py:39
  37.2 1.6 collective-permute-start
  38.7 7.1 %collective-permute-done = bf16[1,128,1024]{1,2,0:T(8,128)(2,1)} collective-permute-done((bf16[1,128,1024]{1,2,0:T(8,128)(2,1)S(1)}, bf16[1,128,1024]{1,2,0:T(8,128)(2,1)}, u32[]{:S(2)}, u32[]{:S(2)}) %collective-permute-start) | collective-permute-done | bytes 262176 | tf_op jit(solution)/shard_map/ppermute | solution.py:16
  45.8 1.1 all-to-all-done
  46.9 4.7 %all-to-all-start.3 = ((bf16[16,64,128]{2,1,0:T(8,128)(2,1)}), bf16[16,64,128]{2,1,0:T(8,128)(2,1)}, u32[]{:S(2)}, u32[]{:S(2)}) async-start(bf16[16,64,128]{2,1,0:T(8,128)(2,1)} %bitcast.13), calls=%async_computation.3 | async-start | bytes 524288 | tf_op jit(solution)/shard_map/all_to_all | solution.py:40
  52.4 9.3 %all-to-all-done.3 = bf16[16,64,128]{2,1,0:T(8,128)(2,1)} async-done(((bf16[16,64,128]{2,1,0:T(8,128)(2,1)}), bf16[16,64,128]{2,1,0:T(8,128)(2,1)}, u32[]{:S(2)}, u32[]{:S(2)}) %all-to-all-start.3) | async-done | bytes 262176 | tf_op jit(solution)/shard_map/all_to_all | solution.py:40
  61.8 58.4 %while.15 = (s32[]{:T(128)}, f32[16,64,128]{2,0,1:T(8,128)}, f32[16,64,128]{2,0,1:T(8,128)}, bf16[4,4,64,128]{3,2,1,0:T(8,128)(2,1)}, s32[4,4]{1,0:T(4,128)}, /*...) while((s32[]{:T(128)}, f32[16,64,128]{2,0,1:T(8,128)}, ...), condition=%wide.region_4.5_spmd.clone, body=%wide.region_0.4_spmd.clone.sunk | while | flops 336365120 | bytes 25971868 | solution.py:127
  63.8 0.7 fusion.89
  66.0 1.3 fusion.94
  67.9 2.3 %convolution_add_fusion.5 = f32[16,64,128]{2,0,1:T(8,128)} fusion(f32[24,64,128]{2,1,0:T(8,128)S(1)} %bitcast.200, f32[16,64,128]{2,0,1:T(8,128)} %get-tuple-element.266, pred[]{:T(512)S(6)} %compare.14, s32[24]{0:T(128)} %eq.43), kind=kOutput, calls=%fused_computation.19.clone.1 | convolution fusion | flops 38011264 | bytes 1835105 | tf_op jit(solution)/shard_map/while/body/eval_jaxpr/tn,nej->tej/dot_general | solution.py:117
  70.2 0.7 gather_fusion.3
  71.0 1.5 fusion.91
  74.2 1.0 convolution_add_fusion.4
  75.1 0.9 fusion.95
  80.2 1.3 fusion.94
  82.2 2.7 %convolution_add_fusion.5 = f32[16,64,128]{2,0,1:T(8,128)} fusion(f32[24,64,128]{2,1,0:T(8,128)S(1)} %bitcast.200, f32[16,64,128]{2,0,1:T(8,128)} %get-tuple-element.266, pred[]{:T(512)S(6)} %compare.14, s32[24]{0:T(128)} %eq.43), kind=kOutput, calls=%fused_computation.19.clone.1 | convolution fusion | flops 38011264 | bytes 1835105 | tf_op jit(solution)/shard_map/while/body/eval_jaxpr/tn,nej->tej/dot_general | solution.py:117
  84.9 0.7 gather_fusion.3
  85.7 1.5 fusion.91
  88.9 1.0 convolution_add_fusion.4
  89.8 0.9 fusion.95
  95.0 1.3 fusion.94
  96.9 2.7 %convolution_add_fusion.5 = f32[16,64,128]{2,0,1:T(8,128)} fusion(f32[24,64,128]{2,1,0:T(8,128)S(1)} %bitcast.200, f32[16,64,128]{2,0,1:T(8,128)} %get-tuple-element.266, pred[]{:T(512)S(6)} %compare.14, s32[24]{0:T(128)} %eq.43), kind=kOutput, calls=%fused_computation.19.clone.1 | convolution fusion | flops 38011264 | bytes 1835105 | tf_op jit(solution)/shard_map/while/body/eval_jaxpr/tn,nej->tej/dot_general | solution.py:117
  99.7 0.7 gather_fusion.3
  100.4 1.5 fusion.91
  103.6 1.0 convolution_add_fusion.4
  104.6 0.9 fusion.95
  109.7 1.3 fusion.94
  111.7 2.7 %convolution_add_fusion.5 = f32[16,64,128]{2,0,1:T(8,128)} fusion(f32[24,64,128]{2,1,0:T(8,128)S(1)} %bitcast.200, f32[16,64,128]{2,0,1:T(8,128)} %get-tuple-element.266, pred[]{:T(512)S(6)} %compare.14, s32[24]{0:T(128)} %eq.43), kind=kOutput, calls=%fused_computation.19.clone.1 | convolution fusion | flops 38011264 | bytes 1835105 | tf_op jit(solution)/shard_map/while/body/eval_jaxpr/tn,nej->tej/dot_general | solution.py:117
  114.4 0.7 gather_fusion.3
  115.1 1.5 fusion.91
  118.3 1.0 convolution_add_fusion.4
  119.3 0.9 fusion.95
  120.2 2.0 %copy.71 = bf16[16,64,128]{2,1,0:T(8,128)(2,1)} copy(f32[16,64,128]{2,0,1:T(8,128)} %get-tuple-element.68) | data formatting | bytes 786432 | tf_op jit(solution)/shard_map/while | solution.py:127
  122.2 3.5 %all-to-all-start.5 = ((bf16[16,1,64,128]{3,2,1,0:T(8,128)(2,1)}), bf16[16,1,64,128]{3,2,1,0:T(8,128)(2,1)S(1)}, u32[]{:S(2)}, u32[]{:S(2)}) async-start(bf16[16,1,64,128]{3,2,1,0:T(8,128)(2,1)} %bitcast.141), calls=%async_computation.5 | async-start | bytes 524288 | tf_op jit(solution)/shard_map/all_to_all | solution.py:153
  125.9 9.8 %all-to-all-done.5 = bf16[16,1,64,128]{3,2,1,0:T(8,128)(2,1)S(1)} async-done(((bf16[16,1,64,128]{3,2,1,0:T(8,128)(2,1)}), bf16[16,1,64,128]{3,2,1,0:T(8,128)(2,1)S(1)}, u32[]{:S(2)}, u32[]{:S(2)}) %all-to-all-start.5) | async-done | bytes 262176 | tf_op jit(solution)/shard_map/all_to_all | solution.py:153
  135.7 12.7 %all_to_all.78 = bf16[16,1,64,128]{3,2,1,0:T(8,128)(2,1)S(1)} all-to-all(bf16[16,1,64,128]{3,2,1,0:T(8,128)(2,1)S(1)} %bitcast.203), channel_id=1, replica_groups=mesh['section'=2,'seq'=16] {'seq'}, dimensions={0} | all-to-all | bytes 524288 | tf_op jit(solution)/shard_map/all_to_all | solution.py:156
  148.4 3.5 %all-to-all-start.4 = ((bf16[16,1,64,128]{3,2,1,0:T(8,128)(2,1)}), bf16[16,1,64,128]{3,2,1,0:T(8,128)(2,1)S(1)}, u32[]{:S(2)}, u32[]{:S(2)}) async-start(bf16[16,1,64,128]{3,2,1,0:T(8,128)(2,1)} %bitcast.18), calls=%async_computation.4 | async-start | bytes 524288 | tf_op jit(solution)/shard_map/all_to_all | solution.py:137
  151.9 0.9 copy.53
  152.8 0.8 copy.54
  153.6 8.3 %all-to-all-done.4 = bf16[16,1,64,128]{3,2,1,0:T(8,128)(2,1)S(1)} async-done(((bf16[16,1,64,128]{3,2,1,0:T(8,128)(2,1)}), bf16[16,1,64,128]{3,2,1,0:T(8,128)(2,1)S(1)}, u32[]{:S(2)}, u32[]{:S(2)}) %all-to-all-start.4) | async-done | bytes 262176 | tf_op jit(solution)/shard_map/all_to_all | solution.py:137
  161.9 0.8 copy.52
  (138 shorter events, 25.9 us)
Async XLA Ops:
  0.6 22.8 %copy-start.6 = (bf16[1,128,1024]{2,1,0:T(8,128)(2,1)S(1)}, bf16[1,128,1024]{2,1,0:T(8,128)(2,1)}, u32[]{:S(2)}) copy-start(bf16[1,128,1024]{2,1,0:T(8,128)(2,1)} %param.8) | copy-start | bytes 786436
  0.6 36.3 %copy-start.7 = (bf16[1,128,1024]{2,1,0:T(8,128)(2,1)S(1)}, bf16[1,128,1024]{2,1,0:T(8,128)(2,1)}, u32[]{:S(2)}) copy-start(bf16[1,128,1024]{2,1,0:T(8,128)(2,1)} %param.11) | copy-start | bytes 786436
  2.5 17.4 %all-to-all-start.1 = ((bf16[16,64,128]{2,1,0:T(8,128)(2,1)}), bf16[16,64,128]{2,1,0:T(8,128)(2,1)S(1)}, u32[]{:S(2)}, u32[]{:S(2)}) async-start(bf16[16,64,128]{2,1,0:T(8,128)(2,1)} %bitcast.8), calls=%async_computation.1 | async-start | bytes 524288 | tf_op jit(solution)/shard_map/all_to_all | solution.py:52
  9.9 41.8 %copy-start.11 = (s32[16,6]{0,1:T(8,128)S(1)}, s32[16,6]{0,1:T(8,128)}, u32[]{:S(2)}) copy-start(s32[16,6]{0,1:T(8,128)} %param.12) | copy-start | bytes 1156
  19.9 13.5 %all-to-all-start.2 = ((bf16[16,64,128]{2,1,0:T(8,128)(2,1)}), bf16[16,64,128]{2,1,0:T(8,128)(2,1)S(1)}, u32[]{:S(2)}, u32[]{:S(2)}) async-start(bf16[16,64,128]{2,1,0:T(8,128)(2,1)} %bitcast.10), calls=%async_computation.2 | async-start | bytes 524288 | tf_op jit(solution)/shard_map/all_to_all | solution.py:53
  33.4 13.5 %all-to-all-start = ((bf16[16,64,128]{2,1,0:T(8,128)(2,1)}), bf16[16,64,128]{2,1,0:T(8,128)(2,1)S(1)}, u32[]{:S(2)}, u32[]{:S(2)}) async-start(bf16[16,64,128]{2,1,0:T(8,128)(2,1)} %bitcast.2), calls=%async_computation | async-start | bytes 524288 | tf_op jit(solution)/shard_map/all_to_all | solution.py:39
  37.2 8.7 %collective-permute-start = (bf16[1,128,1024]{1,2,0:T(8,128)(2,1)S(1)}, bf16[1,128,1024]{1,2,0:T(8,128)(2,1)}, u32[]{:S(2)}, u32[]{:S(2)}) collective-permute-start(bf16[1,128,1024]{1,2,0:T(8,128)(2,1)S(1)} %copy.48), channel_id=1, source_target_pairs={{16,0},{0,16},{17,1},{1,17},{18,2},{2,18},{19,3},{3,19},{20,4},{4,... | collective-permute-start | bytes 786440 | tf_op jit(solution)/shard_map/ppermute | solution.py:16
  46.9 14.8 %all-to-all-start.3 = ((bf16[16,64,128]{2,1,0:T(8,128)(2,1)}), bf16[16,64,128]{2,1,0:T(8,128)(2,1)}, u32[]{:S(2)}, u32[]{:S(2)}) async-start(bf16[16,64,128]{2,1,0:T(8,128)(2,1)} %bitcast.13), calls=%async_computation.3 | async-start | bytes 524288 | tf_op jit(solution)/shard_map/all_to_all | solution.py:40
  63.1 0.6 copy-start.5
  65.6 1.7 %copy-start.3 = (f32[4,128]{1,0:T(4,128)}, f32[4,128]{1,0:T(4,128)S(1)}, u32[]{:S(2)}) copy-start(f32[4,128]{1,0:T(4,128)S(1)} %get-tuple-element.248) | copy-start | bytes 6148 | tf_op jit(solution)/shard_map/while
  66.0 1.4 copy-start.8
  67.9 3.0 %copy-start.4 = (f32[4,128]{1,0:T(4,128)S(1)}, f32[4,128]{1,0:T(4,128)}, u32[]{:S(2)}) copy-start(f32[4,128]{1,0:T(4,128)} %copy-done.3) | copy-start | bytes 6148 | tf_op jit(solution)/shard_map/while
  71.0 1.5 copy-start.9
  73.1 1.0 copy-start
  73.1 1.0 copy-start.10
  75.1 0.9 copy-start.1
  77.4 0.6 copy-start.5
  79.9 1.7 %copy-start.3 = (f32[4,128]{1,0:T(4,128)}, f32[4,128]{1,0:T(4,128)S(1)}, u32[]{:S(2)}) copy-start(f32[4,128]{1,0:T(4,128)S(1)} %get-tuple-element.248) | copy-start | bytes 6148 | tf_op jit(solution)/shard_map/while
  80.2 1.4 copy-start.8
  82.2 3.5 %copy-start.4 = (f32[4,128]{1,0:T(4,128)S(1)}, f32[4,128]{1,0:T(4,128)}, u32[]{:S(2)}) copy-start(f32[4,128]{1,0:T(4,128)} %copy-done.3) | copy-start | bytes 6148 | tf_op jit(solution)/shard_map/while
  85.7 1.5 copy-start.9
  87.8 1.0 copy-start
  87.8 1.0 copy-start.10
  89.8 0.9 copy-start.1
  92.1 0.6 copy-start.5
  94.6 1.7 %copy-start.3 = (f32[4,128]{1,0:T(4,128)}, f32[4,128]{1,0:T(4,128)S(1)}, u32[]{:S(2)}) copy-start(f32[4,128]{1,0:T(4,128)S(1)} %get-tuple-element.248) | copy-start | bytes 6148 | tf_op jit(solution)/shard_map/while
  95.0 1.4 copy-start.8
  96.9 3.5 %copy-start.4 = (f32[4,128]{1,0:T(4,128)S(1)}, f32[4,128]{1,0:T(4,128)}, u32[]{:S(2)}) copy-start(f32[4,128]{1,0:T(4,128)} %copy-done.3) | copy-start | bytes 6148 | tf_op jit(solution)/shard_map/while
  100.4 1.5 copy-start.9
  102.5 1.0 copy-start
  102.6 1.0 copy-start.10
  104.5 0.9 copy-start.1
  106.8 0.6 copy-start.5
  109.3 1.7 %copy-start.3 = (f32[4,128]{1,0:T(4,128)}, f32[4,128]{1,0:T(4,128)S(1)}, u32[]{:S(2)}) copy-start(f32[4,128]{1,0:T(4,128)S(1)} %get-tuple-element.248) | copy-start | bytes 6148 | tf_op jit(solution)/shard_map/while
  109.7 1.4 copy-start.8
  111.7 3.5 %copy-start.4 = (f32[4,128]{1,0:T(4,128)S(1)}, f32[4,128]{1,0:T(4,128)}, u32[]{:S(2)}) copy-start(f32[4,128]{1,0:T(4,128)} %copy-done.3) | copy-start | bytes 6148 | tf_op jit(solution)/shard_map/while
  115.1 1.5 copy-start.9
  117.3 1.0 copy-start
  117.3 1.0 copy-start.10
  119.3 0.9 copy-start.1
  120.2 5.5 %copy-start.2 = (f32[16,64,128]{2,0,1:T(8,128)S(1)}, f32[16,64,128]{2,0,1:T(8,128)}, u32[]{:S(2)}) copy-start(f32[16,64,128]{2,0,1:T(8,128)} %get-tuple-element.69) | copy-start | bytes 1572868
  122.2 13.5 %all-to-all-start.5 = ((bf16[16,1,64,128]{3,2,1,0:T(8,128)(2,1)}), bf16[16,1,64,128]{3,2,1,0:T(8,128)(2,1)S(1)}, u32[]{:S(2)}, u32[]{:S(2)}) async-start(bf16[16,1,64,128]{3,2,1,0:T(8,128)(2,1)} %bitcast.141), calls=%async_computation.5 | async-start | bytes 524288 | tf_op jit(solution)/shard_map/all_to_all | solution.py:153
  148.4 13.5 %all-to-all-start.4 = ((bf16[16,1,64,128]{3,2,1,0:T(8,128)(2,1)}), bf16[16,1,64,128]{3,2,1,0:T(8,128)(2,1)S(1)}, u32[]{:S(2)}, u32[]{:S(2)}) async-start(bf16[16,1,64,128]{3,2,1,0:T(8,128)(2,1)} %bitcast.18), calls=%async_computation.4 | async-start | bytes 524288 | tf_op jit(solution)/shard_map/all_to_all | solution.py:137
where the time goes:
time: 164 us; the launch traced here: 163 us
  waiting for transfers between devices  52.9 us (32%)
  matrix products  33 us (20%)
  starting transfers between devices  27.8 us (17%)
  local copies, waits for them, and re-layouts  24.8 us (15%)
  blocking collectives  12.7 us (8%)
  other arithmetic  10.2 us (6%)
    all_to_all x1, blocking collectives, per_device(): lax.all_to_all(by_source(value_acc).astype(jnp.bfloat16), 'seq', split_ax...  12.7 us
    dot_general x4, matrix products, tile_sweep(): jnp.einsum('tn,nej->tej', picker, value_terms.reshape(-1, DH, TILE), prec...  10.4 us
    all_to_all x1, waiting for transfers between devices, per_device(): lax.all_to_all(by_source(key_acc).astype(jnp.bfloat16), 'seq', split_axis...  9.79 us
    all_to_all x1, waiting for transfers between devices, per_device(): lax.all_to_all(to_slots(adjoint), 'seq', split_axis=0, concat_axis=2, til...  9.33 us
    all_to_all x1, waiting for transfers between devices, per_device(): lax.all_to_all(spread_rows(values), 'seq', split_axis=0, concat_axis=2, t...  9.13 us
    all_to_all x1, waiting for transfers between devices, per_device(): lax.all_to_all(query_send, 'seq', split_axis=0, concat_axis=1, tiled=True)  8.28 us
    all_to_all x1, waiting for transfers between devices, per_device(): lax.all_to_all(spread_rows(keys), 'seq', split_axis=0, concat_axis=2, til...  8.21 us
    all_to_all x1, starting transfers between devices, per_device(): lax.all_to_all(spread_rows(keys), 'seq', split_axis=0, concat_axis=2, til...  7.39 us
  transfers between devices with their start and end apart: 7, of which 7 were waited for; matrix products, arithmetic and copies ran while one was open for 3% of the time, Pallas kernels for 0%

commit v1 on v0

--- a/solution.py
+++ b/solution.py
@@ -134,7 +134,10 @@
         .transpose(0, 2, 1, 3)
         .reshape(seq_count, 1, DH, quarter_rows)
     )
-    query_back = lax.all_to_all(query_send, "seq", split_axis=0, concat_axis=1, tiled=True)
+    query_back = jnp.concatenate(
+        lax.all_to_all(jnp.stack(jnp.split(query_send, lax.axis_size("seq"), axis=0)), "seq", 0, 0),
+        axis=1,
+    )
     query_grad = (
         query_back[0]
         .reshape(group_count, HEADS, DH, quarter_rows)

time: 164 us -> 186 us (1.13); the launches traced: 163 us -> 183 us
  local copies, waits for them, and re-layouts: 24.8 us -> 46.7 us
  blocking collectives: 12.7 us -> 0 us
  waiting for transfers between devices: 52.9 us -> 60.3 us
  starting transfers between devices: 27.8 us -> 31.4 us
    unnamed x16 -> x31, local copies, waits for them, and re-layouts: 7.3 us -> 27.2 us
    all_to_all x1 -> x0, blocking collectives: 12.7 us -> none  [per_device(): lax.all_to_all(by_source(value_acc).astype(jnp.bfloat16), 'seq', split_ax...]
    all_to_all x1 -> x2, waiting for transfers between devices: 8.28 us -> 16.3 us  [the longest x1 8.28 us: per_device(): lax.all_to_all(by_source(value_acc).astype(jnp.bfloat16), 'seq', split_ax...]
    all_to_all x1 -> x2, starting transfers between devices: 3.53 us -> 7.06 us  [the longest x1 3.53 us: per_device(): lax.all_to_all(jnp.stack(jnp.split(query_send, lax.axis_size('seq'), axis...]
  transfers between devices with their start and end apart: 7 -> 8, of which waited for: 7 -> 8; matrix products, arithmetic and copies ran while one was open for 3% -> 4% of each run, Pallas kernels for 0% -> 0%
where the time goes in v1:
time: 186 us; the launch traced here: 183 us
  waiting for transfers between devices  60.3 us (32%)
  local copies, waits for them, and re-layouts  46.7 us (25%)
  matrix products  33 us (18%)
  starting transfers between devices  31.4 us (17%)
  other arithmetic  10.2 us (5%)
    unnamed x31, local copies, waits for them, and re-layouts  27.2 us
    dot_general x4, matrix products, tile_sweep(): jnp.einsum('tn,nej->tej', picker, value_terms.reshape(-1, DH, TILE), prec...  10.4 us
    all_to_all x1, waiting for transfers between devices, per_device(): lax.all_to_all(to_slots(adjoint), 'seq', split_axis=0, concat_axis=2, til...  9.33 us
    all_to_all x1, waiting for transfers between devices, per_device(): lax.all_to_all(spread_rows(values), 'seq', split_axis=0, concat_axis=2, t...  9.13 us
    all_to_all x1, waiting for transfers between devices, per_device(): lax.all_to_all(by_source(key_acc).astype(jnp.bfloat16), 'seq', split_axis...  9.1 us
    all_to_all x1, waiting for transfers between devices, per_device(): lax.all_to_all(by_source(value_acc).astype(jnp.bfloat16), 'seq', split_ax...  8.28 us
    all_to_all x1, waiting for transfers between devices, per_device(): lax.all_to_all(spread_rows(keys), 'seq', split_axis=0, concat_axis=2, til...  8.21 us
    all_to_all x1, waiting for transfers between devices, per_device(): lax.all_to_all(jnp.stack(jnp.split(query_send, lax.axis_size('seq'), axis...  8.06 us
  transfers between devices with their start and end apart: 8, of which 8 were waited for; matrix products, arithmetic and copies ran while one was open for 4% of the time, Pallas kernels for 0%

profile of v1, /device:TPU:0, one launch (start us, length us, event | category | flops | bytes accessed | tf_op | source)
XLA Modules:
  0.0 182.9 jit_solution(11195937883788385844)
XLA Ops:
  0.7 1.8 %copy.61 = bf16[1,128,1024]{1,2,0:T(8,128)(2,1)} copy(bf16[1,128,1024]{2,1,0:T(8,128)(2,1)} %param.9) | data formatting | bytes 524288 | tf_op args[1]
  2.5 7.4 %all-to-all-start.1 = ((bf16[16,64,128]{2,1,0:T(8,128)(2,1)}), bf16[16,64,128]{2,1,0:T(8,128)(2,1)S(1)}, u32[]{:S(2)}, u32[]{:S(2)}) async-start(bf16[16,64,128]{2,1,0:T(8,128)(2,1)} %bitcast.8), calls=%async_computation.1 | async-start | bytes 524288 | tf_op jit(solution)/shard_map/all_to_all | solution.py:52
  9.9 1.8 copy.62
  11.7 8.2 %all-to-all-done.1 = bf16[16,64,128]{2,1,0:T(8,128)(2,1)S(1)} async-done(((bf16[16,64,128]{2,1,0:T(8,128)(2,1)}), bf16[16,64,128]{2,1,0:T(8,128)(2,1)S(1)}, u32[]{:S(2)}, u32[]{:S(2)}) %all-to-all-start.1) | async-done | bytes 262176 | tf_op jit(solution)/shard_map/all_to_all | solution.py:52
  19.9 3.5 %all-to-all-start.2 = ((bf16[16,64,128]{2,1,0:T(8,128)(2,1)}), bf16[16,64,128]{2,1,0:T(8,128)(2,1)S(1)}, u32[]{:S(2)}, u32[]{:S(2)}) async-start(bf16[16,64,128]{2,1,0:T(8,128)(2,1)} %bitcast.10), calls=%async_computation.2 | async-start | bytes 524288 | tf_op jit(solution)/shard_map/all_to_all | solution.py:53
  24.3 9.1 %all-to-all-done.2 = bf16[16,64,128]{2,1,0:T(8,128)(2,1)S(1)} async-done(((bf16[16,64,128]{2,1,0:T(8,128)(2,1)}), bf16[16,64,128]{2,1,0:T(8,128)(2,1)S(1)}, u32[]{:S(2)}, u32[]{:S(2)}) %all-to-all-start.2) | async-done | bytes 262176 | tf_op jit(solution)/shard_map/all_to_all | solution.py:53
  33.4 3.5 %all-to-all-start = ((bf16[16,64,128]{2,1,0:T(8,128)(2,1)}), bf16[16,64,128]{2,1,0:T(8,128)(2,1)S(1)}, u32[]{:S(2)}, u32[]{:S(2)}) async-start(bf16[16,64,128]{2,1,0:T(8,128)(2,1)} %bitcast.2), calls=%async_computation | async-start | bytes 524288 | tf_op jit(solution)/shard_map/all_to_all | solution.py:39
  37.2 1.6 collective-permute-start
  38.7 7.1 %collective-permute-done = bf16[1,128,1024]{1,2,0:T(8,128)(2,1)} collective-permute-done((bf16[1,128,1024]{1,2,0:T(8,128)(2,1)S(1)}, bf16[1,128,1024]{1,2,0:T(8,128)(2,1)}, u32[]{:S(2)}, u32[]{:S(2)}) %collective-permute-start) | collective-permute-done | bytes 262176 | tf_op jit(solution)/shard_map/ppermute | solution.py:16
  45.8 1.1 all-to-all-done
  46.9 4.7 %all-to-all-start.3 = ((bf16[16,64,128]{2,1,0:T(8,128)(2,1)}), bf16[16,64,128]{2,1,0:T(8,128)(2,1)}, u32[]{:S(2)}, u32[]{:S(2)}) async-start(bf16[16,64,128]{2,1,0:T(8,128)(2,1)} %bitcast.13), calls=%async_computation.3 | async-start | bytes 524288 | tf_op jit(solution)/shard_map/all_to_all | solution.py:40
  52.4 9.3 %all-to-all-done.3 = bf16[16,64,128]{2,1,0:T(8,128)(2,1)} async-done(((bf16[16,64,128]{2,1,0:T(8,128)(2,1)}), bf16[16,64,128]{2,1,0:T(8,128)(2,1)}, u32[]{:S(2)}, u32[]{:S(2)}) %all-to-all-start.3) | async-done | bytes 262176 | tf_op jit(solution)/shard_map/all_to_all | solution.py:40
  61.8 58.5 %while.15 = (s32[]{:T(128)}, f32[16,64,128]{2,0,1:T(8,128)}, f32[16,64,128]{2,0,1:T(8,128)}, bf16[4,4,64,128]{3,2,1,0:T(8,128)(2,1)}, s32[4,4]{1,0:T(4,128)}, /*...) while((s32[]{:T(128)}, f32[16,64,128]{2,0,1:T(8,128)}, ...), condition=%wide.region_4.5_spmd.clone, body=%wide.region_0.4_spmd.clone.sunk | while | flops 336365120 | bytes 25971868 | solution.py:127
  66.0 1.3 fusion.94
  67.9 2.3 %convolution_add_fusion.5 = f32[16,64,128]{2,0,1:T(8,128)} fusion(f32[24,64,128]{2,1,0:T(8,128)S(1)} %bitcast.264, f32[16,64,128]{2,0,1:T(8,128)} %get-tuple-element.266, pred[]{:T(512)S(6)} %compare.14, s32[24]{0:T(128)} %eq.43), kind=kOutput, calls=%fused_computation.19.clone.1 | convolution fusion | flops 38011264 | bytes 1835105 | tf_op jit(solution)/shard_map/while/body/eval_jaxpr/tn,nej->tej/dot_general | solution.py:117
  71.0 1.5 fusion.91
  80.3 1.3 fusion.94
  82.2 2.7 %convolution_add_fusion.5 = f32[16,64,128]{2,0,1:T(8,128)} fusion(f32[24,64,128]{2,1,0:T(8,128)S(1)} %bitcast.264, f32[16,64,128]{2,0,1:T(8,128)} %get-tuple-element.266, pred[]{:T(512)S(6)} %compare.14, s32[24]{0:T(128)} %eq.43), kind=kOutput, calls=%fused_computation.19.clone.1 | convolution fusion | flops 38011264 | bytes 1835105 | tf_op jit(solution)/shard_map/while/body/eval_jaxpr/tn,nej->tej/dot_general | solution.py:117
  85.7 1.5 fusion.91
  95.0 1.3 fusion.94
  97.0 2.7 %convolution_add_fusion.5 = f32[16,64,128]{2,0,1:T(8,128)} fusion(f32[24,64,128]{2,1,0:T(8,128)S(1)} %bitcast.264, f32[16,64,128]{2,0,1:T(8,128)} %get-tuple-element.266, pred[]{:T(512)S(6)} %compare.14, s32[24]{0:T(128)} %eq.43), kind=kOutput, calls=%fused_computation.19.clone.1 | convolution fusion | flops 38011264 | bytes 1835105 | tf_op jit(solution)/shard_map/while/body/eval_jaxpr/tn,nej->tej/dot_general | solution.py:117
  100.5 1.5 fusion.91
  109.7 1.3 fusion.94
  111.7 2.7 %convolution_add_fusion.5 = f32[16,64,128]{2,0,1:T(8,128)} fusion(f32[24,64,128]{2,1,0:T(8,128)S(1)} %bitcast.264, f32[16,64,128]{2,0,1:T(8,128)} %get-tuple-element.266, pred[]{:T(512)S(6)} %compare.14, s32[24]{0:T(128)} %eq.43), kind=kOutput, calls=%fused_computation.19.clone.1 | convolution fusion | flops 38011264 | bytes 1835105 | tf_op jit(solution)/shard_map/while/body/eval_jaxpr/tn,nej->tej/dot_general | solution.py:117
  115.2 1.5 fusion.91
  120.2 1.4 constant_dynamic-update-slice_fusion.15
  121.6 1.3 constant_dynamic-update-slice_fusion.14
  123.0 1.3 constant_dynamic-update-slice_fusion.13
  124.3 1.3 constant_dynamic-update-slice_fusion.12
  125.6 1.3 constant_dynamic-update-slice_fusion.11
  126.9 1.3 constant_dynamic-update-slice_fusion.10
  128.2 1.3 constant_dynamic-update-slice_fusion.9
  129.6 1.3 constant_dynamic-update-slice_fusion.8
  130.9 1.3 constant_dynamic-update-slice_fusion.7
  132.2 1.3 constant_dynamic-update-slice_fusion.6
  133.5 1.3 constant_dynamic-update-slice_fusion.5
  134.9 1.3 constant_dynamic-update-slice_fusion.4
  136.2 1.3 constant_dynamic-update-slice_fusion.3
  137.5 1.3 constant_dynamic-update-slice_fusion.2
  138.8 1.3 constant_dynamic-update-slice_fusion.1
  140.2 1.3 constant_dynamic-update-slice_fusion
  141.5 3.5 %all-to-all-start.4 = ((bf16[16,1,1,64,128]{4,3,2,1,0:T(8,128)(2,1)}), bf16[16,1,1,64,128]{4,3,2,1,0:T(8,128)(2,1)S(1)}, u32[]{:S(2)}, u32[]{:S(2)}) async-start(bf16[16,1,1,64,128]{4,3,2,1,0:T(8,128)(2,1)} %constant_dynamic-update-slice_fusion), calls=%async_computation.4 | async-start | bytes 524288 | tf_op jit(solution)/shard_map/all_to_all | solution.py:138
  145.0 1.9 %copy.86 = bf16[16,64,128]{2,1,0:T(8,128)(2,1)} copy(f32[16,64,128]{2,0,1:T(8,128)} %get-tuple-element.68) | data formatting | bytes 786432 | tf_op jit(solution)/shard_map/while | solution.py:127
  146.9 8.1 %all-to-all-done.4 = bf16[16,1,1,64,128]{4,3,2,1,0:T(8,128)(2,1)S(1)} async-done(((bf16[16,1,1,64,128]{4,3,2,1,0:T(8,128)(2,1)}), bf16[16,1,1,64,128]{4,3,2,1,0:T(8,128)(2,1)S(1)}, u32[]{:S(2)}, u32[]{:S(2)}) %all-to-all-start.4) | async-done | bytes 262176 | tf_op jit(solution)/shard_map/all_to_all | solution.py:138
  155.0 3.5 %all-to-all-start.5 = ((bf16[16,1,64,128]{3,2,1,0:T(8,128)(2,1)}), bf16[16,1,64,128]{3,2,1,0:T(8,128)(2,1)S(1)}, u32[]{:S(2)}, u32[]{:S(2)}) async-start(bf16[16,1,64,128]{3,2,1,0:T(8,128)(2,1)} %bitcast.205), calls=%async_computation.5 | async-start | bytes 524288 | tf_op jit(solution)/shard_map/all_to_all | solution.py:156
  159.4 9.1 %all-to-all-done.5 = bf16[16,1,64,128]{3,2,1,0:T(8,128)(2,1)S(1)} async-done(((bf16[16,1,64,128]{3,2,1,0:T(8,128)(2,1)}), bf16[16,1,64,128]{3,2,1,0:T(8,128)(2,1)S(1)}, u32[]{:S(2)}, u32[]{:S(2)}) %all-to-all-start.5) | async-done | bytes 262176 | tf_op jit(solution)/shard_map/all_to_all | solution.py:156
  168.5 3.5 %all-to-all-start.6 = ((bf16[16,1,64,128]{3,2,1,0:T(8,128)(2,1)}), bf16[16,1,64,128]{3,2,1,0:T(8,128)(2,1)S(1)}, u32[]{:S(2)}, u32[]{:S(2)}) async-start(bf16[16,1,64,128]{3,2,1,0:T(8,128)(2,1)} %bitcast.206), calls=%async_computation.6 | async-start | bytes 524288 | tf_op jit(solution)/shard_map/all_to_all | solution.py:159
  173.8 8.3 %all-to-all-done.6 = bf16[16,1,64,128]{3,2,1,0:T(8,128)(2,1)S(1)} async-done(((bf16[16,1,64,128]{3,2,1,0:T(8,128)(2,1)}), bf16[16,1,64,128]{3,2,1,0:T(8,128)(2,1)S(1)}, u32[]{:S(2)}, u32[]{:S(2)}) %all-to-all-start.6) | async-done | bytes 262176 | tf_op jit(solution)/shard_map/all_to_all | solution.py:159
  (155 shorter events, 41.3 us)
Async XLA Ops:
  0.6 22.8 %copy-start.6 = (bf16[1,128,1024]{2,1,0:T(8,128)(2,1)S(1)}, bf16[1,128,1024]{2,1,0:T(8,128)(2,1)}, u32[]{:S(2)}) copy-start(bf16[1,128,1024]{2,1,0:T(8,128)(2,1)} %param.8) | copy-start | bytes 786436
  0.6 36.3 %copy-start.7 = (bf16[1,128,1024]{2,1,0:T(8,128)(2,1)S(1)}, bf16[1,128,1024]{2,1,0:T(8,128)(2,1)}, u32[]{:S(2)}) copy-start(bf16[1,128,1024]{2,1,0:T(8,128)(2,1)} %param.11) | copy-start | bytes 786436
  2.5 17.4 %all-to-all-start.1 = ((bf16[16,64,128]{2,1,0:T(8,128)(2,1)}), bf16[16,64,128]{2,1,0:T(8,128)(2,1)S(1)}, u32[]{:S(2)}, u32[]{:S(2)}) async-start(bf16[16,64,128]{2,1,0:T(8,128)(2,1)} %bitcast.8), calls=%async_computation.1 | async-start | bytes 524288 | tf_op jit(solution)/shard_map/all_to_all | solution.py:52
  9.9 41.8 %copy-start.11 = (s32[16,6]{0,1:T(8,128)S(1)}, s32[16,6]{0,1:T(8,128)}, u32[]{:S(2)}) copy-start(s32[16,6]{0,1:T(8,128)} %param.12) | copy-start | bytes 1156
  19.9 13.5 %all-to-all-start.2 = ((bf16[16,64,128]{2,1,0:T(8,128)(2,1)}), bf16[16,64,128]{2,1,0:T(8,128)(2,1)S(1)}, u32[]{:S(2)}, u32[]{:S(2)}) async-start(bf16[16,64,128]{2,1,0:T(8,128)(2,1)} %bitcast.10), calls=%async_computation.2 | async-start | bytes 524288 | tf_op jit(solution)/shard_map/all_to_all | solution.py:53
  33.4 13.5 %all-to-all-start = ((bf16[16,64,128]{2,1,0:T(8,128)(2,1)}), bf16[16,64,128]{2,1,0:T(8,128)(2,1)S(1)}, u32[]{:S(2)}, u32[]{:S(2)}) async-start(bf16[16,64,128]{2,1,0:T(8,128)(2,1)} %bitcast.2), calls=%async_computation | async-start | bytes 524288 | tf_op jit(solution)/shard_map/all_to_all | solution.py:39
  37.2 8.7 %collective-permute-start = (bf16[1,128,1024]{1,2,0:T(8,128)(2,1)S(1)}, bf16[1,128,1024]{1,2,0:T(8,128)(2,1)}, u32[]{:S(2)}, u32[]{:S(2)}) collective-permute-start(bf16[1,128,1024]{1,2,0:T(8,128)(2,1)S(1)} %copy.63), channel_id=1, source_target_pairs={{16,0},{0,16},{17,1},{1,17},{18,2},{2,18},{19,3},{3,19},{20,4},{4,... | collective-permute-start | bytes 786440 | tf_op jit(solution)/shard_map/ppermute | solution.py:16
  46.9 14.8 %all-to-all-start.3 = ((bf16[16,64,128]{2,1,0:T(8,128)(2,1)}), bf16[16,64,128]{2,1,0:T(8,128)(2,1)}, u32[]{:S(2)}, u32[]{:S(2)}) async-start(bf16[16,64,128]{2,1,0:T(8,128)(2,1)} %bitcast.13), calls=%async_computation.3 | async-start | bytes 524288 | tf_op jit(solution)/shard_map/all_to_all | solution.py:40
  63.1 0.6 copy-start.5
  65.6 1.7 copy-start.3
  66.0 1.4 copy-start.8
  67.9 3.0 %copy-start.4 = (f32[4,128]{1,0:T(4,128)S(1)}, f32[4,128]{1,0:T(4,128)}, u32[]{:S(2)}) copy-start(f32[4,128]{1,0:T(4,128)} %copy-done.3) | copy-start | bytes 6148 | tf_op jit(solution)/shard_map/while
  71.0 1.5 copy-start.9
  73.1 1.0 copy-start
  73.1 1.0 copy-start.10
  75.1 0.9 copy-start.1
  77.4 0.6 copy-start.5
  79.9 1.7 copy-start.3
  80.3 1.4 copy-start.8
  82.2 3.5 %copy-start.4 = (f32[4,128]{1,0:T(4,128)S(1)}, f32[4,128]{1,0:T(4,128)}, u32[]{:S(2)}) copy-start(f32[4,128]{1,0:T(4,128)} %copy-done.3) | copy-start | bytes 6148 | tf_op jit(solution)/shard_map/while
  85.7 1.5 copy-start.9
  87.8 1.0 copy-start
  87.9 1.0 copy-start.10
  89.9 0.9 copy-start.1
  92.1 0.6 copy-start.5
  94.6 1.7 copy-start.3
  95.0 1.4 copy-start.8
  97.0 3.5 %copy-start.4 = (f32[4,128]{1,0:T(4,128)S(1)}, f32[4,128]{1,0:T(4,128)}, u32[]{:S(2)}) copy-start(f32[4,128]{1,0:T(4,128)} %copy-done.3) | copy-start | bytes 6148 | tf_op jit(solution)/shard_map/while
  100.4 1.5 copy-start.9
  102.6 1.0 copy-start
  102.6 1.0 copy-start.10
  104.6 0.9 copy-start.1
  106.9 0.6 copy-start.5
  109.3 1.7 copy-start.3
  109.7 1.4 copy-start.8
  111.7 3.5 %copy-start.4 = (f32[4,128]{1,0:T(4,128)S(1)}, f32[4,128]{1,0:T(4,128)}, u32[]{:S(2)}) copy-start(f32[4,128]{1,0:T(4,128)} %copy-done.3) | copy-start | bytes 6148 | tf_op jit(solution)/shard_map/while
  115.2 1.5 copy-start.9
  117.3 1.0 copy-start
  117.3 1.0 copy-start.10
  119.3 0.9 copy-start.1
  120.2 38.3 %copy-start.2 = (f32[16,64,128]{2,0,1:T(8,128)S(1)}, f32[16,64,128]{2,0,1:T(8,128)}, u32[]{:S(2)}) copy-start(f32[16,64,128]{2,0,1:T(8,128)} %get-tuple-element.69) | copy-start | bytes 1572868
  141.5 13.5 %all-to-all-start.4 = ((bf16[16,1,1,64,128]{4,3,2,1,0:T(8,128)(2,1)}), bf16[16,1,1,64,128]{4,3,2,1,0:T(8,128)(2,1)S(1)}, u32[]{:S(2)}, u32[]{:S(2)}) async-start(bf16[16,1,1,64,128]{4,3,2,1,0:T(8,128)(2,1)} %constant_dynamic-update-slice_fusion), calls=%async_computation.4 | async-start | bytes 524288 | tf_op jit(solution)/shard_map/all_to_all | solution.py:138
  155.0 13.5 %all-to-all-start.5 = ((bf16[16,1,64,128]{3,2,1,0:T(8,128)(2,1)}), bf16[16,1,64,128]{3,2,1,0:T(8,128)(2,1)S(1)}, u32[]{:S(2)}, u32[]{:S(2)}) async-start(bf16[16,1,64,128]{3,2,1,0:T(8,128)(2,1)} %bitcast.205), calls=%async_computation.5 | async-start | bytes 524288 | tf_op jit(solution)/shard_map/all_to_all | solution.py:156
  168.5 13.5 %all-to-all-start.6 = ((bf16[16,1,64,128]{3,2,1,0:T(8,128)(2,1)}), bf16[16,1,64,128]{3,2,1,0:T(8,128)(2,1)S(1)}, u32[]{:S(2)}, u32[]{:S(2)}) async-start(bf16[16,1,64,128]{3,2,1,0:T(8,128)(2,1)} %bitcast.206), calls=%async_computation.6 | async-start | bytes 524288 | tf_op jit(solution)/shard_map/all_to_all | solution.py:159
